TPU v7x, 512 devices: a whole 4x8x8 slice. The times are simulated.
512 devices in a mesh: seq: 64 (over x, z, core), head: 8 (over y).
Axes of the slice: x: 4, y: 8, z: 8, core: 2. Of those that a mesh axis runs over, the one named last changes fastest.
Arguments:
- queries: bfloat16 [16384, 4096], P('seq', 'head'), may hold values from -6 to 6
- keys: bfloat16 [16384, 4096], P('seq', 'head'), may hold values from -6 to 6
- values: bfloat16 [16384, 4096], P('seq', 'head'), may hold values from -6 to 6
- gate: bfloat16 [16384, 4096], P('seq', 'head'), may hold values from -6 to 6
- residual: bfloat16 [16384, 4096], P('seq', 'head'), may hold values from -40 to 40
- log_decay: float32 [16384, 32], P('seq', 'head'), may hold values from -1 to 0, as said below
- out_weight: bfloat16 [4096, 4096], P('seq', 'head'), may hold values from -0.09375 to 0.09375
- norm_gain: bfloat16 [4096], P('head'), may hold values from 0.099609375 to 1.8984375
- kv_weight: bfloat16 [4096, 2048], P('seq', 'head'), may hold values from -0.09375 to 0.09375
Outputs:
- cache_keys: bfloat16 [16384, 1024], P('seq', 'head')
- cache_values: bfloat16 [16384, 1024], P('seq', 'head')
Inputs may be any that keep to these rules, and one draw needn't show every extreme that they name: `log_decay`: every entry is negative.
All inputs are finite; a program needn't handle non-finite values.
Results may differ from a plain program's by a relative error of at most 0.015.
Values may be sent and summed in bfloat16 or wider, within the bound.
A program may use at most 64 MiB of HBM per device.

v0:
```python
import jax
import jax.numpy as jnp
from jax import lax
from jax.sharding import PartitionSpec as P

HIGHEST = lax.Precision.HIGHEST


def entering(part, axis, combine, identity):
    place = lax.axis_index(axis)
    gathered = jax.tree.map(lambda a: lax.all_gather(a, axis), part)
    state = jax.tree.map(lambda a, e: jnp.zeros_like(a) + jnp.asarray(e, a.dtype), part, identity)

    def one(step, state):
        return combine(
            state, jax.tree.map(lambda a: lax.dynamic_index_in_dim(a, step, 0, False), gathered)
        )

    return lax.fori_loop(0, place, one, state)


def local_retention(queries, keys, values, log_decay, block):
    tokens, heads, width = queries.shape
    count = tokens // block

    def to_blocks(array):
        return array.reshape((count, block) + array.shape[1:])

    lower = jnp.arange(block)[:, None] >= jnp.arange(block)[None, :]

    def advance(carry, inputs):
        state, offset = carry
        query_block, key_block, value_block, decay_block = inputs
        within = jnp.cumsum(decay_block, axis=0)
        spread = within[:, None, :] - within[None, :, :]
        factor = jnp.where(
            lower[:, :, None], jnp.exp(jnp.where(lower[:, :, None], spread, 0.0)), 0.0
        )
        scores = jnp.einsum(
            "ihd,jhd->hij", query_block, key_block, preferred_element_type=jnp.float32
        )
        weighted = scores * jnp.transpose(factor, (2, 0, 1))
        values_wide = value_block.astype(jnp.float32)
        intra = jnp.einsum("hij,jhd->ihd", weighted, values_wide, precision=HIGHEST)
        query_wide = query_block.astype(jnp.float32)
        carried = jnp.exp(within)[:, :, None] * jnp.einsum(
            "ihd,hde->ihe", query_wide, state, precision=HIGHEST
        )
        ending = within[-1]
        key_wide = key_block.astype(jnp.float32) * jnp.exp(ending[None, :] - within)[:, :, None]
        fresh = jnp.exp(ending)[:, None, None] * state + jnp.einsum(
            "jhd,jhe->hde", key_wide, values_wide, precision=HIGHEST
        )
        return ((fresh, offset + ending), (intra + carried, offset[None, :] + within))

    start = (jnp.zeros((heads, width, width), jnp.float32), jnp.zeros((heads,), jnp.float32))
    final, stacked = lax.scan(
        advance,
        start,
        (to_blocks(queries), to_blocks(keys), to_blocks(values), to_blocks(log_decay)),
    )
    return (
        stacked[0].reshape(tokens, heads, width),
        stacked[1].reshape(tokens, heads),
        final[0],
        final[1],
    )


def combine_states(earlier, later):
    return (earlier[0] * later[0], later[0][:, None, None] * earlier[1] + later[1])


def on_device(queries, keys, values, gate, residual, log_decay, out_weight, norm_gain, kv_weight):
    tokens = queries.shape[0]
    heads = log_decay.shape[1]
    width = queries.shape[1] // heads
    shaped = [array.reshape(tokens, heads, width) for array in (queries, keys, values)]
    partial_out, running, state, offset = local_retention(
        shaped[0], shaped[1], shaped[2], log_decay, min(512, tokens)
    )
    identity = (jnp.ones((heads,), jnp.float32), jnp.zeros((heads, width, width), jnp.float32))
    scan_decay, incoming = entering((jnp.exp(offset), state), "seq", combine_states, identity)
    retained = partial_out + jnp.exp(running)[:, :, None] * jnp.einsum(
        "thd,hde->the", shaped[0].astype(jnp.float32), incoming, precision=HIGHEST
    )
    scale = lax.rsqrt(jnp.mean(retained * retained, axis=2, keepdims=True) + 1e-06)
    mixed = (
        jax.nn.silu(gate.astype(jnp.float32)) * (retained * scale).reshape(tokens, heads * width)
    ).astype(jnp.bfloat16)
    all_heads = lax.all_gather(mixed, "head", axis=1, tiled=True)
    out_full, kv_full = (
        lax.all_gather(out_weight, "seq", axis=0, tiled=True),
        lax.all_gather(kv_weight, "seq", axis=0, tiled=True),
    )
    branch = jnp.dot(all_heads, out_full, preferred_element_type=jnp.float32)
    hidden = (residual.astype(jnp.float32) + branch).astype(jnp.bfloat16)
    wide = hidden.astype(jnp.float32)
    squares = lax.psum(jnp.sum(wide * wide, axis=1), "head")
    features = wide.shape[1] * lax.axis_size("head")
    inverse = lax.rsqrt(squares[:, None] / features + 1e-06)
    local_norm = (wide * inverse * norm_gain.astype(jnp.float32)[None, :]).astype(jnp.bfloat16)
    normalized = lax.all_gather(local_norm, "head", axis=1, tiled=True)
    projected = jnp.dot(normalized, kv_full, preferred_element_type=jnp.float32)
    cache_heads = kv_weight.shape[1] // (2 * width)
    arranged = projected.reshape(tokens, cache_heads, 2, width)
    cache_keys = arranged[:, :, 0, :].reshape(tokens, cache_heads * width).astype(jnp.bfloat16)
    cache_values = arranged[:, :, 1, :].reshape(tokens, cache_heads * width).astype(jnp.bfloat16)
    return (cache_keys, cache_values)


def solution(mesh):
    placed = (
        P("seq", "head"),
        P("seq", "head"),
        P("seq", "head"),
        P("seq", "head"),
        P("seq", "head"),
        P("seq", "head"),
        P("seq", "head"),
        P("head"),
        P("seq", "head"),
    )
    return jax.shard_map(
        on_device,
        mesh=mesh,
        in_specs=placed,
        out_specs=(P("seq", "head"), P("seq", "head")),
        check_vma=False,
    )
```

profile of v0, /device:TPU:2, one launch (start us, length us, event | category | flops | bytes accessed | tf_op | source)
XLA Modules:
  0.0 390.9 jit_solution(8764286394529594663)
XLA Ops:
  8.0 1.2 reduce-window.6
  9.8 1.1 copy.73
  10.9 2.0 convolution_add_fusion.1
  13.8 44.7 %all-gather.1 = f32[64,1,4]{2,1,0:T(1,128)S(1)} all-gather(f32[1,1,4]{2,1,0:T(1,128)S(1)} %bitcast.97), channel_id=1, replica_groups=mesh['seq'=64,'head'=8] {'seq'}, dimensions={0}, use_global_device_ids=true | all-gather | bytes 1040 | tf_op jit(solution)/shard_map/all_gather | solution.py:11
  59.4 63.1 %all-gather.16.cloned.1.call-done = f32[256,128,128]{2,1,0:T(8,128)} async-done(((f32[4,128,128]{2,1,0:T(8,128)}), f32[256,128,128]{2,1,0:T(8,128)}) %all-gather.16.cloned.1.call-update) | async-done | bytes 16777232 | tf_op jit(solution)/shard_map/all_gather | solution.py:11
  122.5 17.8 %while.3 = (s32[]{:T(128)}, f32[4,128,128]{2,1,0:T(8,128)S(1)}, s32[]{:T(128)}, f32[64,4]{1,0:T(8,128)S(1)}, f32[64,4,128,128]{3,2,1,0:T(8,128)}, /*index=5*/s32[]{:T(128)}, s32[]{:T(128)}, s32[]{:T(128)}) while((s32[]{:T(128)}, f32[4,128,128]{2,1,0:T(8,128)S(1)}, s32[]{:T(128)}, f32[64,4]{1,0:T(8,128)S(1)}, f32[64,4,128,128]{3,2,1,0:T(8,128)}, ...), condition=%wide.region_3.4_spmd, body=%wide.region_2.3_spmd.sunk | while | flops 131077 | bytes 786607 | solution.py:19
  122.6 1.1 bitcast_add_fusion.2
  123.7 1.1 bitcast_add_fusion.2
  124.8 1.1 bitcast_add_fusion.2
  125.9 1.1 bitcast_add_fusion.2
  127.0 1.1 bitcast_add_fusion.2
  128.1 1.1 bitcast_add_fusion.2
  129.2 1.1 bitcast_add_fusion.2
  130.4 1.1 bitcast_add_fusion.2
  137.0 1.1 bitcast_add_fusion.2
  138.1 1.1 bitcast_add_fusion.2
  139.2 1.1 bitcast_add_fusion.2
  143.4 64.4 %all-gather.10.cloned.1.call-done = bf16[4096,512]{1,0:T(8,128)(2,1)} async-done(((bf16[64,512]{1,0:T(8,128)(2,1)}), bf16[4096,512]{1,0:T(8,128)(2,1)}) %all-gather.10.cloned.1.call-update) | async-done | bytes 4194320 | tf_op jit(solution)/shard_map/all_gather | solution.py:93
  207.8 43.4 %all-gather.8.cloned.1.call-done = bf16[256,4096]{1,0:T(8,128)(2,1)} async-done(((bf16[256,512]{1,0:T(8,128)(2,1)}), bf16[256,4096]{1,0:T(8,128)(2,1)}) %all-gather.8.cloned.1.call-update) | async-done | bytes 2097168 | tf_op jit(solution)/shard_map/all_gather | solution.py:91
  251.2 4.2 %multiply_reduce_fusion = (f32[256]{0:T(256)S(1)}, f32[256,512]{1,0:T(8,128)S(1)}) fusion(bf16[256,4096]{1,0:T(8,128)(2,1)} %all-gather.8.cloned.1.call-done, bf16[4096,512]{1,0:T(8,128)(2,1)} %all-gather.10.cloned.1.call-done, bf16[256,512]{1,0:T(8,128)(2,1)S(1)} %copy-done.4), kind=kOutput, calls=%fused_computation.22 | convolution fusion | flops 1074528000 | bytes 7078912 | tf_op jit(solution)/shard_map/dot_general | solution.py:96
  255.3 16.2 %psum.7 = f32[256]{0:T(256)S(1)} all-reduce(f32[256]{0:T(256)S(1)} %get-tuple-element.97), channel_id=1, replica_groups=mesh['seq'=64,'head'=8] {'head'}, use_global_device_ids=true, to_apply=%region_6.7 | all-reduce | flops 256 | bytes 2048 | tf_op jit(solution)/shard_map/psum | solution.py:99
  272.4 63.8 %all-gather.14.cloned.1.call-done = bf16[4096,256]{1,0:T(8,128)(2,1)} async-done(((bf16[64,256]{1,0:T(8,128)(2,1)}), bf16[4096,256]{1,0:T(8,128)(2,1)}) %all-gather.14.cloned.1.call-update) | async-done | bytes 2097168 | tf_op jit(solution)/shard_map/all_gather | solution.py:94
  336.2 43.6 %all-gather.12.cloned.1.call-done = bf16[256,4096]{1,0:T(8,128)(2,1)} async-done(((bf16[256,512]{1,0:T(8,128)(2,1)}), bf16[256,4096]{1,0:T(8,128)(2,1)}) %all-gather.12.cloned.1.call-update) | async-done | bytes 2097168 | tf_op jit(solution)/shard_map/all_gather | solution.py:103
  379.8 3.1 convolution_convert_fusion
  (68 shorter events, 13.8 us)
Async XLA Ops:
  7.2 51.4 %copy-start = (bf16[256,512]{1,0:T(8,128)(2,1)S(1)}, bf16[256,512]{1,0:T(8,128)(2,1)}, u32[]{:S(2)}) copy-start(bf16[256,512]{1,0:T(8,128)(2,1)} %param.11) | copy-start | bytes 786436
  7.2 115.3 %all-gather.16.cloned.1.call-start = ((), (), s32[]{:S(2)}) async-start(), calls=%async_computation.4 | async-start | bytes 17039360 | tf_op jit(solution)/shard_map/all_gather | solution.py:11
  13.0 194.8 %all-gather.10.cloned.1.call-start = ((), (), s32[]{:S(2)}) async-start(), calls=%async_computation.1 | async-start | bytes 4259840 | tf_op jit(solution)/shard_map/all_gather | solution.py:93
  13.8 237.4 %all-gather.8.cloned.1.call-start = ((), (), s32[]{:S(2)}) async-start(), calls=%async_computation | async-start | bytes 2359296 | tf_op jit(solution)/shard_map/all_gather | solution.py:91
  122.5 18.2 %copy-start.1 = (bf16[256,512]{1,0:T(8,128)(2,1)S(1)}, bf16[256,512]{1,0:T(8,128)(2,1)}, u32[]{:S(2)}) copy-start(bf16[256,512]{1,0:T(8,128)(2,1)} %param.13) | copy-start | bytes 786436
  140.8 1.1 copy-start.2
  141.5 1.8 copy-start.3
  141.5 109.7 %copy-start.4 = (bf16[256,512]{1,0:T(8,128)(2,1)S(1)}, bf16[256,512]{1,0:T(8,128)(2,1)}, u32[]{:S(2)}) copy-start(bf16[256,512]{1,0:T(8,128)(2,1)} %param.15) | copy-start | bytes 786436
  142.7 193.4 %all-gather.14.cloned.1.call-start = ((), (), s32[]{:S(2)}) async-start(), calls=%async_computation.3 | async-start | bytes 2129920 | tf_op jit(solution)/shard_map/all_gather | solution.py:94
  143.3 236.5 %all-gather.12.cloned.1.call-start = ((), (), s32[]{:S(2)}) async-start(), calls=%async_computation.2 | async-start | bytes 2359296 | tf_op jit(solution)/shard_map/all_gather | solution.py:103
Sparse Core Ops, SparseCore 0:
  13.1 109.3 all-gather.15
  125.8 81.8 all-gather.9
  209.9 41.2 all-gather.7
  254.4 81.7 all-gather.13
  338.1 41.6 all-gather.11
where the time goes:
time: 393 us; the launch traced here: 391 us
  waiting for transfers between devices  280 us (71%)
  blocking collectives  60.9 us (15%)
  other arithmetic  20.2 us (5%)
  between operations  14 us (4%)
  matrix products  11.3 us (3%)
  local copies, waits for them, and re-layouts  4.19 us (1%)
    all_gather x1, waiting for transfers between devices, on_device(): lax.all_gather(out_weight, 'seq', axis=0, tiled=True)  64.4 us
    all_gather x1, waiting for transfers between devices, on_device(): lax.all_gather(kv_weight, 'seq', axis=0, tiled=True)  63.8 us
    all_gather x1, waiting for transfers between devices, entering(): gathered = jax.tree.map(lambda a: lax.all_gather(a, axis), part)  63.1 us
    all_gather x1, blocking collectives, entering(): gathered = jax.tree.map(lambda a: lax.all_gather(a, axis), part)  44.7 us
    all_gather x1, waiting for transfers between devices, on_device(): normalized = lax.all_gather(local_norm, 'head', axis=1, tiled=True)  43.6 us
    all_gather x1, waiting for transfers between devices, on_device(): all_heads = lax.all_gather(mixed, 'head', axis=1, tiled=True)  43.4 us
    add x16, other arithmetic, combine_states(): later[0][:, None, None] * earlier[1] + later[1]  17 us
    psum x1, blocking collectives, on_device(): squares = lax.psum(jnp.sum(wide * wide, axis=1), 'head')  16.2 us
  transfers between devices with their start and end apart: 5, of which 5 were waited for; matrix products, arithmetic and copies ran while one was open for 6% of the time, Pallas kernels for 0%

commit v1 on v0

--- a/solution.py
+++ b/solution.py
@@ -4,6 +4,12 @@
 from jax.sharding import PartitionSpec as P
 
 HIGHEST = lax.Precision.HIGHEST
+
+
+def gather_by_exchange(x, axis, dim):
+    peers = lax.axis_size(axis)
+    repeats = [peers if d == dim else 1 for d in range(x.ndim)]
+    return lax.all_to_all(jnp.tile(x, repeats), axis, split_axis=dim, concat_axis=dim, tiled=True)
 
 
 def entering(part, axis, combine, identity):
@@ -91,7 +97,7 @@
     all_heads = lax.all_gather(mixed, "head", axis=1, tiled=True)
     out_full, kv_full = (
         lax.all_gather(out_weight, "seq", axis=0, tiled=True),
-        lax.all_gather(kv_weight, "seq", axis=0, tiled=True),
+        gather_by_exchange(kv_weight, "seq", 0),
     )
     branch = jnp.dot(all_heads, out_full, preferred_element_type=jnp.float32)
     hidden = (residual.astype(jnp.float32) + branch).astype(jnp.bfloat16)

time: 393 us -> 329 us (0.84)
  waiting for transfers between devices: 280 us -> 155 us
  starting transfers between devices: 0.2 us -> 57.5 us
    all_gather x1 -> x0, waiting for transfers between devices: 63.8 us -> none  [on_device(): lax.all_gather(kv_weight, 'seq', axis=0, tiled=True)]
    all_to_all x0 -> x1, starting transfers between devices: none -> 57.3 us  [gather_by_exchange(): lax.all_to_all(jnp.tile(x, repeats), axis, split_axis=dim, concat_axis=di...]
    all_gather x1, waiting for transfers between devices: 64.4 us -> 7.22 us  [on_device(): lax.all_gather(out_weight, 'seq', axis=0, tiled=True)]
  transfers between devices with their start and end apart: 5 -> 5, of which waited for: 5 -> 4; matrix products, arithmetic and copies ran while one was open for 6% -> 9% of each run, Pallas kernels for 0% -> 0%
where the time goes in v1:
time: 329 us; the launch traced here: 327 us
  waiting for transfers between devices  155 us (47%)
  blocking collectives  60.7 us (18%)
  starting transfers between devices  57.5 us (17%)
  other arithmetic  20.2 us (6%)
  between operations  14 us (4%)
  matrix products  11.1 us (3%)
  local copies, waits for them, and re-layouts  7.91 us (2%)
    all_gather x1, waiting for transfers between devices, entering(): gathered = jax.tree.map(lambda a: lax.all_gather(a, axis), part)  63.1 us
    all_to_all x1, starting transfers between devices, gather_by_exchange(): lax.all_to_all(jnp.tile(x, repeats), axis, split_axis=dim, concat_axis=di...  57.3 us
    all_gather x1, blocking collectives, entering(): gathered = jax.tree.map(lambda a: lax.all_gather(a, axis), part)  44.7 us
    all_gather x1, waiting for transfers between devices, on_device(): all_heads = lax.all_gather(mixed, 'head', axis=1, tiled=True)  43.8 us
    all_gather x1, waiting for transfers between devices, on_device(): normalized = lax.all_gather(local_norm, 'head', axis=1, tiled=True)  40 us
    add x16, other arithmetic, combine_states(): later[0][:, None, None] * earlier[1] + later[1]  17 us
    psum x1, blocking collectives, on_device(): squares = lax.psum(jnp.sum(wide * wide, axis=1), 'head')  16 us
    all_gather x1, waiting for transfers between devices, on_device(): lax.all_gather(out_weight, 'seq', axis=0, tiled=True)  7.22 us
  transfers between devices with their start and end apart: 5, of which 4 were waited for; matrix products, arithmetic and copies ran while one was open for 9% of the time, Pallas kernels for 0%

profile of v1, /device:TPU:2, one launch (start us, length us, event | category | flops | bytes accessed | tf_op | source)
XLA Modules:
  0.0 326.8 jit_solution(12163116581943568174)
XLA Ops:
  8.0 1.2 reduce-window.6
  9.8 1.1 copy.83
  10.9 2.0 convolution_add_fusion.1
  13.8 44.7 %all-gather.1 = f32[64,1,4]{2,1,0:T(1,128)S(1)} all-gather(f32[1,1,4]{2,1,0:T(1,128)S(1)} %bitcast.109), channel_id=1, replica_groups=mesh['seq'=64,'head'=8] {'seq'}, dimensions={0}, use_global_device_ids=true | all-gather | bytes 1040 | tf_op jit(solution)/shard_map/all_gather | solution.py:17
  59.4 63.1 %all-gather.13.cloned.1.call-done = f32[256,128,128]{2,1,0:T(8,128)} async-done(((f32[4,128,128]{2,1,0:T(8,128)}), f32[256,128,128]{2,1,0:T(8,128)}) %all-gather.13.cloned.1.call-update) | async-done | bytes 16777232 | tf_op jit(solution)/shard_map/all_gather | solution.py:17
  122.5 17.8 %while.3 = (s32[]{:T(128)}, f32[4,128,128]{2,1,0:T(8,128)S(1)}, s32[]{:T(128)}, f32[64,4]{1,0:T(8,128)S(1)}, f32[64,4,128,128]{3,2,1,0:T(8,128)}, /*index=5*/s32[]{:T(128)}, s32[]{:T(128)}, s32[]{:T(128)}) while((s32[]{:T(128)}, f32[4,128,128]{2,1,0:T(8,128)S(1)}, s32[]{:T(128)}, f32[64,4]{1,0:T(8,128)S(1)}, f32[64,4,128,128]{3,2,1,0:T(8,128)}, ...), condition=%wide.region_3.4_spmd, body=%wide.region_2.3_spmd.sunk | while | flops 131077 | bytes 786607 | solution.py:25
  122.6 1.1 bitcast_add_fusion.2
  123.7 1.1 bitcast_add_fusion.2
  124.8 1.1 bitcast_add_fusion.2
  125.9 1.1 bitcast_add_fusion.2
  127.0 1.1 bitcast_add_fusion.2
  128.1 1.1 bitcast_add_fusion.2
  129.2 1.1 bitcast_add_fusion.2
  138.1 1.1 bitcast_add_fusion.2
  139.2 1.1 bitcast_add_fusion.2
  142.7 1.6 tile.2
  144.3 57.3 %all-to-all-start = ((bf16[64,64,256]{2,1,0:T(8,128)(2,1)}), bf16[64,64,256]{2,1,0:T(8,128)(2,1)S(1)}, u32[]{:S(2)}, u32[]{:S(2)}) async-start(bf16[64,64,256]{2,1,0:T(8,128)(2,1)} %tile.2), calls=%async_computation | async-start | bytes 4194304 | tf_op jit(solution)/shard_map/all_to_all | solution.py:12
  201.7 7.2 %all-gather.9.cloned.1.call-done = bf16[4096,512]{1,0:T(8,128)(2,1)} async-done(((bf16[64,512]{1,0:T(8,128)(2,1)}), bf16[4096,512]{1,0:T(8,128)(2,1)}) %all-gather.9.cloned.1.call-update) | async-done | bytes 4194320 | tf_op jit(solution)/shard_map/all_gather | solution.py:99
  208.9 43.8 %all-gather.7.cloned.1.call-done = bf16[256,4096]{1,0:T(8,128)(2,1)} async-done(((bf16[256,512]{1,0:T(8,128)(2,1)}), bf16[256,4096]{1,0:T(8,128)(2,1)}) %all-gather.7.cloned.1.call-update) | async-done | bytes 2097168 | tf_op jit(solution)/shard_map/all_gather | solution.py:97
  252.7 4.1 %multiply_reduce_fusion = (f32[256]{0:T(256)S(1)}, f32[256,512]{1,0:T(8,128)S(1)}) fusion(bf16[256,4096]{1,0:T(8,128)(2,1)} %all-gather.7.cloned.1.call-done, bf16[4096,512]{1,0:T(8,128)(2,1)} %all-gather.9.cloned.1.call-done, bf16[256,512]{1,0:T(8,128)(2,1)S(1)} %copy-done.5), kind=kOutput, calls=%fused_computation.25 | convolution fusion | flops 1074528000 | bytes 7078912 | tf_op jit(solution)/shard_map/dot_general | solution.py:102
  256.8 16.0 %psum.7 = f32[256]{0:T(256)S(1)} all-reduce(f32[256]{0:T(256)S(1)} %get-tuple-element.97), channel_id=1, replica_groups=mesh['seq'=64,'head'=8] {'head'}, use_global_device_ids=true, to_apply=%region_6.7 | all-reduce | flops 256 | bytes 2048 | tf_op jit(solution)/shard_map/psum | solution.py:105
  273.7 2.9 copy.80
  276.6 40.0 %all-gather.11.cloned.1.call-done = bf16[256,4096]{1,0:T(8,128)(2,1)} async-done(((bf16[256,512]{1,0:T(8,128)(2,1)}), bf16[256,4096]{1,0:T(8,128)(2,1)}) %all-gather.11.cloned.1.call-update) | async-done | bytes 2097168 | tf_op jit(solution)/shard_map/all_gather | solution.py:109
  316.7 3.0 fusion.11
  (69 shorter events, 14.5 us)
Async XLA Ops:
  7.2 51.4 %copy-start = (bf16[256,512]{1,0:T(8,128)(2,1)S(1)}, bf16[256,512]{1,0:T(8,128)(2,1)}, u32[]{:S(2)}) copy-start(bf16[256,512]{1,0:T(8,128)(2,1)} %param.11) | copy-start | bytes 786436
  7.2 115.3 %all-gather.13.cloned.1.call-start = ((), (), s32[]{:S(2)}) async-start(), calls=%async_computation.4 | async-start | bytes 17039360 | tf_op jit(solution)/shard_map/all_gather | solution.py:17
  13.0 195.9 %all-gather.9.cloned.1.call-start = ((), (), s32[]{:S(2)}) async-start(), calls=%async_computation.2 | async-start | bytes 4259840 | tf_op jit(solution)/shard_map/all_gather | solution.py:99
  13.8 238.9 %all-gather.7.cloned.1.call-start = ((), (), s32[]{:S(2)}) async-start(), calls=%async_computation.1 | async-start | bytes 2359296 | tf_op jit(solution)/shard_map/all_gather | solution.py:97
  122.5 18.2 %copy-start.1 = (bf16[256,512]{1,0:T(8,128)(2,1)S(1)}, bf16[256,512]{1,0:T(8,128)(2,1)}, u32[]{:S(2)}) copy-start(bf16[256,512]{1,0:T(8,128)(2,1)} %param.13) | copy-start | bytes 786436
  140.7 1.1 copy-start.2
  141.5 1.2 copy-start.3
  144.3 57.4 %copy-start.4 = (bf16[512]{0:T(512)(128)(2,1)S(1)}, bf16[512]{0:T(512)(128)(2,1)}, u32[]{:S(2)}) copy-start(bf16[512]{0:T(512)(128)(2,1)} %param.18) | copy-start | bytes 3076
  144.3 108.4 %copy-start.5 = (bf16[256,512]{1,0:T(8,128)(2,1)S(1)}, bf16[256,512]{1,0:T(8,128)(2,1)}, u32[]{:S(2)}) copy-start(bf16[256,512]{1,0:T(8,128)(2,1)} %param.15) | copy-start | bytes 786436
  144.3 129.4 %all-to-all-start = ((bf16[64,64,256]{2,1,0:T(8,128)(2,1)}), bf16[64,64,256]{2,1,0:T(8,128)(2,1)S(1)}, u32[]{:S(2)}, u32[]{:S(2)}) async-start(bf16[64,64,256]{2,1,0:T(8,128)(2,1)} %tile.2), calls=%async_computation | async-start | bytes 4194304 | tf_op jit(solution)/shard_map/all_to_all | solution.py:12
  201.6 115.1 %all-gather.11.cloned.1.call-start = ((), (), s32[]{:S(2)}) async-start(), calls=%async_computation.3 | async-start | bytes 2359296 | tf_op jit(solution)/shard_map/all_gather | solution.py:109
Sparse Core Ops, SparseCore 0:
  13.1 109.3 all-gather.12
  125.8 82.9 all-gather.8
  211.0 41.6 all-gather.6
  273.8 42.8 all-gather.10
